TPU v7x, 32 devices: a whole 2x2x4 slice. The times are simulated.
32 devices in a mesh: grp: 4 (over x, core), dev: 8 (over z, y).
Axes of the slice: x: 2, y: 2, z: 4, core: 2. Of those that a mesh axis runs over, the one named last changes fastest.
Arguments:
- features: bfloat16 [24576, 512], P(('grp', 'dev')), may hold values from -6 to 6
- grad_out: bfloat16 [24576, 512], P(('grp', 'dev')), may hold values from -6 to 6
- w_self: bfloat16 [512, 512], replicated, may hold values from -0.25 to 0.25
- w_neigh: bfloat16 [512, 512], replicated, may hold values from -0.25 to 0.25
- neighbours: int32 [24576, 32], P(('grp', 'dev')), may hold values from 0 to 895, as said below
- degree: int32 [24576], P(('grp', 'dev')), may hold values from 8 to 32
- send_rows: int32 [256, 8], P(('grp', 'dev')), may hold values from 0 to 767
- hub_rows: int32 [64], P(('grp', 'dev')), may hold values from 0 to 767, as said below
Outputs:
- output: bfloat16 [24576, 512], P(('grp', 'dev'))
- grad_features: bfloat16 [24576, 512], P(('grp', 'dev'))
Inputs may be any that keep to these rules, and one draw needn't show every extreme that they name: `neighbours`: codes below 768 name rows of the node's device, the next 64 name rows listed for it by its group, the last 64 name hub nodes. Slot 0 of every node holds a listed row and slot 1 a hub; every listed row of a device is named by some node of the reading device and every hub by some node. `hub_rows`: the 2 entries of one device are distinct rows of that device.
All inputs are finite; a program needn't handle non-finite values.
Results may differ from a plain program's by a relative error of at most 0.0051.
Values may be sent and summed in bfloat16 or wider, within the bound.
A program may use at most 64 MiB of HBM per device.

v0:
```python
import math
import jax
import jax.numpy as jnp
from jax import lax
from jax.sharding import PartitionSpec as P


def count_tiles(slot_codes, keep_mask, tile_width, first_code):
    column_ids = first_code + lax.iota(jnp.int32, tile_width)
    matches = (slot_codes[:, :, None] == column_ids[None, None, :]) & keep_mask[:, :, None]
    return jnp.sum(matches.astype(jnp.bfloat16), axis=1)


def local(features, grad_out, w_self, w_neigh, neighbours, degree, send_rows, hub_rows):
    row_count, feat_width = features.shape
    slot_count = neighbours.shape[1]
    groups = lax.axis_size("grp")
    members = lax.axis_size("dev")
    halo_count = send_rows.shape[0] * send_rows.shape[1]
    owned_hubs = hub_rows.shape[0]
    hub_count = owned_hubs * groups * members
    keep_slots = lax.iota(jnp.int32, slot_count)[None, :] < degree[:, None]
    block_rows = math.gcd(row_count, 256)
    block_total = row_count // block_rows

    def build_tiles(block_args):
        slot_codes, keep_mask = block_args
        return (
            count_tiles(slot_codes, keep_mask, row_count, 0),
            count_tiles(slot_codes, keep_mask, halo_count, row_count),
            count_tiles(slot_codes, keep_mask, hub_count, row_count + halo_count),
        )

    tile_local, tile_halo, tile_hub = lax.map(
        build_tiles,
        (
            neighbours.reshape(block_total, block_rows, slot_count),
            keep_slots.reshape(block_total, block_rows, slot_count),
        ),
    )
    tile_local = tile_local.reshape(row_count, row_count)
    tile_halo = tile_halo.reshape(row_count, halo_count)
    tile_hub = tile_hub.reshape(row_count, hub_count)
    send_list = send_rows.reshape(halo_count)
    outgoing = jnp.take(features, send_list, axis=0)
    incoming = lax.all_to_all(outgoing, "dev", split_axis=0, concat_axis=0, tiled=True)
    summed = jnp.dot(tile_local, features, preferred_element_type=jnp.float32)
    summed = summed + jnp.dot(tile_halo, incoming, preferred_element_type=jnp.float32)
    hub_own = jnp.take(features, hub_rows, axis=0)
    tile_cols = tile_hub
    summed = summed + jnp.dot(
        tile_cols,
        lax.all_gather(hub_own, ("grp", "dev"), axis=0, tiled=True),
        preferred_element_type=jnp.float32,
    )
    degree_f = degree.astype(jnp.float32)[:, None]
    neigh_mean = (summed / degree_f).astype(jnp.bfloat16)
    preact = jnp.dot(features, w_self, preferred_element_type=jnp.float32) + jnp.dot(
        neigh_mean, w_neigh, preferred_element_type=jnp.float32
    )
    output = jax.nn.silu(preact).astype(jnp.bfloat16)
    sigmoid_pre = jax.nn.sigmoid(preact)
    gated = (
        grad_out.astype(jnp.float32) * sigmoid_pre * (1.0 + preact * (1.0 - sigmoid_pre))
    ).astype(jnp.bfloat16)
    contract_last = (((1,), (1,)), ((), ()))
    contract_first = (((0,), (0,)), ((), ()))
    grad_self = lax.dot_general(gated, w_self, contract_last, preferred_element_type=jnp.float32)
    scaled = (
        lax.dot_general(gated, w_neigh, contract_last, preferred_element_type=jnp.float32)
        / degree_f
    ).astype(jnp.bfloat16)
    grad_total = grad_self + lax.dot_general(
        tile_local, scaled, contract_first, preferred_element_type=jnp.float32
    )
    halo_partial = lax.dot_general(
        tile_halo, scaled, contract_first, preferred_element_type=jnp.float32
    )
    returned = lax.all_to_all(
        halo_partial.astype(jnp.bfloat16), "dev", split_axis=0, concat_axis=0, tiled=True
    ).astype(halo_partial.dtype)
    grad_total = grad_total + jax.ops.segment_sum(returned, send_list, num_segments=row_count)
    tile_cols = tile_hub
    mine = lax.psum_scatter(
        lax.dot_general(tile_cols, scaled, contract_first, preferred_element_type=jnp.float32),
        ("grp", "dev"),
        scatter_dimension=0,
        tiled=True,
    )
    grad_total = grad_total + jax.ops.segment_sum(mine, hub_rows, num_segments=row_count)
    return (output, grad_total.astype(jnp.bfloat16))


def solution(mesh):
    placed = (
        P(("grp", "dev"), None),
        P(("grp", "dev"), None),
        P(),
        P(),
        P(("grp", "dev"), None),
        P(("grp", "dev")),
        P(("grp", "dev"), None),
        P(("grp", "dev")),
    )
    return jax.shard_map(
        local,
        mesh=mesh,
        in_specs=placed,
        out_specs=(P(("grp", "dev"), None), P(("grp", "dev"), None)),
        check_vma=False,
    )
```

profile of v0, /device:TPU:0, one launch (start us, length us, event | category | flops | bytes accessed | tf_op | source)
XLA Modules:
  0.0 273.5 jit_solution(13714239355453946839)
XLA Ops:
  7.2 0.0 copy-start
  7.2 0.8 reshape.95
  8.0 0.7 compare_and_fusion
  8.7 0.0 copy-done
  8.7 0.7 gather_fusion
  9.4 0.7 bitcast_select_fusion
  10.1 7.3 %all-to-all-start = ((bf16[8,8,512]{2,1,0:T(8,128)(2,1)}), bf16[8,8,512]{2,1,0:T(8,128)(2,1)S(1)}, u32[]{:S(2)}, u32[]{:S(2)}) async-start(bf16[8,8,512]{2,1,0:T(8,128)(2,1)} %bitcast_select_fusion), calls=%async_computation | async-start | bytes 131072 | tf_op jit(solution)/shard_map/all_to_all | solution.py:46
  17.5 0.7 compare_select_fusion.1
  18.1 0.7 compare_and_fusion.1
  18.8 0.9 reshape.92
  19.7 0.7 lt.49
  20.5 23.6 %while.17 = (s32[]{:T(128)}, bf16[3,256,768]{2,1,0:T(8,128)(2,1)S(1)}, bf16[3,256,64]{1,2,0:T(8,128)(2,1)S(1)}, bf16[3,256,64]{1,2,0:T(8,128)(2,1)S(1)}, s32[3,2...) while((s32[]{:T(128)}, bf16[3,256,768]{2,1,0:T(8,128)(2,1)S(1)}, ...), condition=%wide.region_4.5_spmd, body=%wide.region_0.4_spmd.sunk | while | flops 29130880 | bytes 1688669 | solution.py:34
  20.6 0.8 fusion.40
  21.4 0.1 copy.28
  21.5 0.1 copy.29
  21.6 6.7 %fusion.39 = bf16[256,768]{1,0:T(8,128)(2,1)S(1)} fusion(s32[256,32]{1,0:T(8,128)S(1)} %bitcast.64, pred[256,32]{1,0:T(8,128)(4,1)S(1)} %copy.29), kind=kLoop, calls=%fused_computation.6.clone.1 | loop fusion | flops 24969216 | bytes 434176 | tf_op jit(solution)/shard_map/while/body/eval_jaxpr/reduce_sum | solution.py:11
  28.4 0.8 fusion.40
  29.2 0.1 copy.28
  29.3 0.1 copy.29
  29.5 6.7 %fusion.39 = bf16[256,768]{1,0:T(8,128)(2,1)S(1)} fusion(s32[256,32]{1,0:T(8,128)S(1)} %bitcast.64, pred[256,32]{1,0:T(8,128)(4,1)S(1)} %copy.29), kind=kLoop, calls=%fused_computation.6.clone.1 | loop fusion | flops 24969216 | bytes 434176 | tf_op jit(solution)/shard_map/while/body/eval_jaxpr/reduce_sum | solution.py:11
  36.3 0.8 fusion.40
  37.1 0.1 copy.28
  37.2 0.1 copy.29
  37.3 6.7 %fusion.39 = bf16[256,768]{1,0:T(8,128)(2,1)S(1)} fusion(s32[256,32]{1,0:T(8,128)S(1)} %bitcast.64, pred[256,32]{1,0:T(8,128)(4,1)S(1)} %copy.29), kind=kLoop, calls=%fused_computation.6.clone.1 | loop fusion | flops 24969216 | bytes 434176 | tf_op jit(solution)/shard_map/while/body/eval_jaxpr/reduce_sum | solution.py:11
  44.1 0.0 copy-start.3
  44.1 1.0 copy-done.3
  45.1 0.0 copy-start.1
  45.1 1.9 fusion.16
  47.1 0.0 copy-done.1
  47.1 0.0 copy-start.2
  47.1 0.0 copy-start.5
  47.1 1.7 fusion.15
  48.8 0.6 gather_fusion.1
  49.4 0.1 fusion.13
  49.5 68.1 %all-gather = bf16[32,2,512]{2,1,0:T(2,128)(2,1)S(1)} all-gather(bf16[1,2,512]{2,1,0:T(2,128)(2,1)S(1)} %fusion.13), channel_id=1, replica_groups=mesh['grp'=4,'dev'=8] {'grp','dev'}, dimensions={0}, use_global_device_ids=true | all-gather | bytes 67584 | tf_op jit(solution)/shard_map/all_gather | solution.py:53
  117.6 0.0 copy-done.2
  117.7 0.0 copy-done.5
  117.7 0.1 add_bitcast_fusion
  117.7 0.0 all-to-all-done
  117.7 0.4 fusion.11
  118.1 4.9 %multiply_convert_fusion = (bf16[768,512]{1,0:T(8,128)(2,1)}, bf16[768,512]{1,0:T(8,128)(2,1)}) fusion(bf16[768,512]{1,0:T(8,128)(2,1)} %param.11, f32[768,512]{1,0:T(8,128)} %fusion.15, bf16[512,512]{1,0:T(8,128)(2,1)} %param.13, f32[768,512]{1,0:T(8,128)} %fusion.16, f32[768,512]{1,0:T(8,128)S(1)} %fusion.11, bf16[768,64]{0,1:T(8,128)(2,1)S(1)} %bitcast.68, ...), kind=kOutput, calls=%fused_computation.20 | convolution fusion | flops 459669504 | bytes 7769088 | tf_op jit(solution)/shard_map/dot_general | solution.py:58
  123.0 0.0 copy-start.4
  123.0 2.0 divide_convert_fusion
  125.0 0.0 copy-done.4
  125.0 2.0 fusion.17
  127.0 0.9 fusion.5
  127.9 0.9 fusion.18
  128.8 3.3 %all-to-all-start.1 = ((bf16[8,8,512]{2,1,0:T(8,128)(2,1)}), bf16[8,8,512]{2,1,0:T(8,128)(2,1)S(1)}, u32[]{:S(2)}, u32[]{:S(2)}) async-start(bf16[8,8,512]{2,1,0:T(8,128)(2,1)} %fusion.5), calls=%async_computation.1 | async-start | bytes 131072 | tf_op jit(solution)/shard_map/all_to_all | solution.py:79
  132.1 0.0 all-reduce.3.cloned.1.call-start
  132.2 0.7 all-reduce.3.cloned.1.call-update
  132.9 2.3 convolution_add_fusion
  135.1 128.2 %all-reduce.3.cloned.1.call-done = f32[64,512]{1,0:T(8,128)} async-done(((f32[64,512]{1,0:T(8,128)}), f32[64,512]{1,0:T(8,128)}) %all-reduce.3.cloned.1.call-update) | async-done | bytes 131088
  263.4 0.7 constant_dynamic-slice_fusion.1
  264.1 0.0 all-to-all-done.1
  264.1 1.6 scatter_custom_fusion
  265.7 1.0 convert_element_type.66
  (33 shorter events, 0.4 us)
Async XLA Ops:
  7.2 1.6 copy-start
  10.1 107.6 %all-to-all-start = ((bf16[8,8,512]{2,1,0:T(8,128)(2,1)}), bf16[8,8,512]{2,1,0:T(8,128)(2,1)S(1)}, u32[]{:S(2)}, u32[]{:S(2)}) async-start(bf16[8,8,512]{2,1,0:T(8,128)(2,1)} %bitcast_select_fusion), calls=%async_computation | async-start | bytes 131072 | tf_op jit(solution)/shard_map/all_to_all | solution.py:46
  44.1 1.0 copy-start.3
  45.1 1.9 copy-start.1
  47.1 70.5 %copy-start.2 = (s32[768]{0:T(1024)S(1)}, s32[768]{0:T(1024)}, u32[]{:S(2)}) copy-start(s32[768]{0:T(1024)} %param.15) | copy-start | bytes 9220
  47.1 70.6 %copy-start.5 = (s32[2]{0:T(128)S(1)}, s32[2]{0:T(128)}, u32[]{:S(2)}) copy-start(s32[2]{0:T(128)} %param.17) | copy-start | bytes 28
  123.0 2.0 copy-start.4
  128.8 135.3 %all-to-all-start.1 = ((bf16[8,8,512]{2,1,0:T(8,128)(2,1)}), bf16[8,8,512]{2,1,0:T(8,128)(2,1)S(1)}, u32[]{:S(2)}, u32[]{:S(2)}) async-start(bf16[8,8,512]{2,1,0:T(8,128)(2,1)} %fusion.5), calls=%async_computation.1 | async-start | bytes 131072 | tf_op jit(solution)/shard_map/all_to_all | solution.py:79
  132.1 131.2 %all-reduce.3.cloned.1.call-start = ((), (), s32[]{:S(2)}) async-start(), calls=%async_computation.2 | async-start | bytes 262144
Sparse Core Ops, SparseCore 0:
  138.5 124.8 all-reduce.2
where the time goes:
time: 274 us
  waiting for transfers between devices  129 us (47%)
  blocking collectives  68.1 us (25%)
  other arithmetic  27.9 us (10%)
  matrix products  16.9 us (6%)
  between operations  14.2 us (5%)
  starting transfers between devices  10.7 us (4%)
  local copies, waits for them, and re-layouts  6.51 us (2%)
    unnamed x2, waiting for transfers between devices  129 us
    all_gather x1, blocking collectives, local(): lax.all_gather(hub_own, ('grp', 'dev'), axis=0, tiled=True)  68.1 us
    reduce_sum x6, other arithmetic, count_tiles(): return jnp.sum(matches.astype(jnp.bfloat16), axis=1)  22.4 us
    all_to_all x1, starting transfers between devices, local(): lax.all_to_all(outgoing, 'dev', split_axis=0, concat_axis=0, tiled=True)  7.31 us
  transfers between devices with their start and end apart: 3, of which 1 were waited for; matrix products, arithmetic and copies ran while one was open for 12% of the time, Pallas kernels for 0%

commit v1 on v0

--- a/solution.py
+++ b/solution.py
@@ -3,6 +3,18 @@
 import jax.numpy as jnp
 from jax import lax
 from jax.sharding import PartitionSpec as P
+
+
+def doubled_up(value, axis, dim):
+    ways, here, turn = (lax.axis_size(axis), lax.axis_index(axis), value.shape[dim])
+    line, have = (value, 1)
+    while have < ways:
+        line = jnp.concatenate(
+            [line, lax.ppermute(line, axis, [(d, (d - have) % ways) for d in range(ways)])],
+            axis=dim,
+        )
+        have = 2 * have
+    return jnp.roll(line, here * turn, axis=dim)
 
 
 def count_tiles(slot_codes, keep_mask, tile_width, first_code):
@@ -49,9 +61,7 @@
     hub_own = jnp.take(features, hub_rows, axis=0)
     tile_cols = tile_hub
     summed = summed + jnp.dot(
-        tile_cols,
-        lax.all_gather(hub_own, ("grp", "dev"), axis=0, tiled=True),
-        preferred_element_type=jnp.float32,
+        tile_cols, doubled_up(hub_own, ("grp", "dev"), 0), preferred_element_type=jnp.float32
     )
     degree_f = degree.astype(jnp.float32)[:, None]
     neigh_mean = (summed / degree_f).astype(jnp.bfloat16)

time: 274 us -> 219 us (0.80)
  blocking collectives: 68.1 us -> 0 us
  starting transfers between devices: 10.7 us -> 17.7 us
  waiting for transfers between devices: 129 us -> 134 us
    all_gather x1 -> x0, blocking collectives: 68.1 us -> none  [local(): lax.all_gather(hub_own, ('grp', 'dev'), axis=0, tiled=True)]
    ppermute x0 -> x5, starting transfers between devices: none -> 11 us  [doubled_up(): lax.ppermute(line, axis, [(d, (d - have) % ways) for d in range(ways)])]
    ppermute x0 -> x5, waiting for transfers between devices: none -> 4.91 us  [doubled_up(): lax.ppermute(line, axis, [(d, (d - have) % ways) for d in range(ways)])]
    all_to_all x1, starting transfers between devices: 7.31 us -> 3.35 us  [local(): lax.all_to_all(outgoing, 'dev', split_axis=0, concat_axis=0, tiled=True)]
  transfers between devices with their start and end apart: 3 -> 8, of which waited for: 1 -> 3; matrix products, arithmetic and copies ran while one was open for 12% -> 16% of each run, Pallas kernels for 0% -> 0%
where the time goes in v1:
time: 219 us
  waiting for transfers between devices  134 us (61%)
  other arithmetic  28 us (13%)
  matrix products  18.1 us (8%)
  starting transfers between devices  17.7 us (8%)
  between operations  14.2 us (6%)
  local copies, waits for them, and re-layouts  6.37 us (3%)
    unnamed x2, waiting for transfers between devices  129 us
    reduce_sum x6, other arithmetic, count_tiles(): return jnp.sum(matches.astype(jnp.bfloat16), axis=1)  22.3 us
    ppermute x5, starting transfers between devices, doubled_up(): lax.ppermute(line, axis, [(d, (d - have) % ways) for d in range(ways)])  11 us
    ppermute x5, waiting for transfers between devices, doubled_up(): lax.ppermute(line, axis, [(d, (d - have) % ways) for d in range(ways)])  4.91 us
    dot_general x1, matrix products, local(): jnp.dot(neigh_mean, w_neigh, preferred_element_type=jnp.float32)  4.86 us
  transfers between devices with their start and end apart: 8, of which 3 were waited for; matrix products, arithmetic and copies ran while one was open for 16% of the time, Pallas kernels for 0%

profile of v1, /device:TPU:0, one launch (start us, length us, event | category | flops | bytes accessed | tf_op | source)
XLA Modules:
  0.0 218.8 jit_solution(13168533487759379695)
XLA Ops:
  7.2 0.0 copy-start
  7.2 0.7 compare_select_fusion.1
  7.9 0.7 compare_and_fusion.1
  8.6 0.0 copy-done
  8.6 0.6 gather_fusion.1
  9.2 0.1 broadcast_select_fusion
  9.2 6.4 %collective-permute-start = (bf16[2,512]{1,0:T(2,128)(2,1)S(1)}, bf16[2,512]{1,0:T(2,128)(2,1)S(1)}, u32[]{:S(2)}, u32[]{:S(2)}) collective-permute-start(bf16[2,512]{1,0:T(2,128)(2,1)S(1)} %broadcast_select_fusion), channel_id=1, source_target_pairs={{0,31},{1,0},{2,1},{3,2},{4,3},{5,4},{6,5},{7,6},{8,7},{9,8},{10,9... | collective-permute-start | bytes 6152 | tf_op jit(solution)/shard_map/ppermute | solution.py:13
  15.6 0.8 reshape.95
  16.4 0.7 compare_and_fusion
  17.1 0.7 gather_fusion
  17.8 0.7 bitcast_select_fusion
  18.5 3.4 %all-to-all-start = ((bf16[8,8,512]{2,1,0:T(8,128)(2,1)}), bf16[8,8,512]{2,1,0:T(8,128)(2,1)S(1)}, u32[]{:S(2)}, u32[]{:S(2)}) async-start(bf16[8,8,512]{2,1,0:T(8,128)(2,1)} %bitcast_select_fusion), calls=%async_computation | async-start | bytes 131072 | tf_op jit(solution)/shard_map/all_to_all | solution.py:58
  21.9 0.7 lt.61
  22.6 0.9 reshape.92
  23.6 0.0 collective-permute-done
  23.6 3.8 %collective-permute-start.1 = (bf16[4,512]{1,0:T(4,128)(2,1)S(1)}, bf16[4,512]{1,0:T(4,128)(2,1)S(1)}, u32[]{:S(2)}, u32[]{:S(2)}) collective-permute-start(bf16[4,512]{1,0:T(4,128)(2,1)S(1)} %pad_maximum_fusion.2), channel_id=1, source_target_pairs={{0,30},{1,31},{2,0},{3,1},{4,2},{5,3},{6,4},{7,5},{8,6},{9,7},{10,... | collective-permute-start | bytes 12296 | tf_op jit(solution)/shard_map/ppermute | solution.py:13
  27.4 23.5 %while.17 = (s32[]{:T(128)}, bf16[3,256,768]{2,1,0:T(8,128)(2,1)S(1)}, bf16[3,256,64]{1,2,0:T(8,128)(2,1)S(1)}, bf16[3,256,64]{1,2,0:T(8,128)(2,1)S(1)}, s32[3,2...) while((s32[]{:T(128)}, bf16[3,256,768]{2,1,0:T(8,128)(2,1)S(1)}, ...), condition=%wide.region_4.5_spmd, body=%wide.region_0.4_spmd.sunk | while | flops 29130880 | bytes 1688669 | solution.py:46
  27.5 0.8 fusion.44
  28.3 0.1 copy.28
  28.4 0.1 copy.29
  28.5 6.7 %fusion.43 = bf16[256,768]{1,0:T(8,128)(2,1)S(1)} fusion(s32[256,32]{1,0:T(8,128)S(1)} %bitcast.61, pred[256,32]{1,0:T(8,128)(4,1)S(1)} %copy.29), kind=kLoop, calls=%fused_computation.6.clone.1 | loop fusion | flops 24969216 | bytes 434176 | tf_op jit(solution)/shard_map/while/body/eval_jaxpr/reduce_sum | solution.py:23
  35.4 0.8 fusion.44
  36.1 0.1 copy.28
  36.2 0.1 copy.29
  36.4 6.7 %fusion.43 = bf16[256,768]{1,0:T(8,128)(2,1)S(1)} fusion(s32[256,32]{1,0:T(8,128)S(1)} %bitcast.61, pred[256,32]{1,0:T(8,128)(4,1)S(1)} %copy.29), kind=kLoop, calls=%fused_computation.6.clone.1 | loop fusion | flops 24969216 | bytes 434176 | tf_op jit(solution)/shard_map/while/body/eval_jaxpr/reduce_sum | solution.py:23
  43.2 0.8 fusion.44
  44.0 0.1 copy.28
  44.1 0.1 copy.29
  44.2 6.7 %fusion.43 = bf16[256,768]{1,0:T(8,128)(2,1)S(1)} fusion(s32[256,32]{1,0:T(8,128)S(1)} %bitcast.61, pred[256,32]{1,0:T(8,128)(4,1)S(1)} %copy.29), kind=kLoop, calls=%fused_computation.6.clone.1 | loop fusion | flops 24969216 | bytes 434176 | tf_op jit(solution)/shard_map/while/body/eval_jaxpr/reduce_sum | solution.py:23
  51.0 0.0 copy-start.3
  51.0 0.0 collective-permute-done.1
  51.0 0.1 collective-permute-start.2
  51.1 0.9 copy-done.3
  52.0 0.0 copy-start.1
  52.0 1.9 fusion.21
  53.9 0.0 copy-start.4
  53.9 0.0 copy-start.2
  53.9 1.7 collective-permute-done.2
  55.6 0.1 collective-permute-start.3
  55.7 0.0 copy-done.1
  55.7 1.7 fusion.20
  57.4 0.0 collective-permute-done.3
  57.5 0.6 collective-permute-start.4
  58.1 0.0 copy-done.4
  58.1 0.1 add_bitcast_fusion
  58.2 0.0 copy-done.2
  58.2 3.2 %collective-permute-done.4 = bf16[32,512]{1,0:T(8,128)(2,1)S(1)} collective-permute-done((bf16[32,512]{1,0:T(8,128)(2,1)S(1)}, bf16[32,512]{1,0:T(8,128)(2,1)S(1)}, u32[]{:S(2)}, u32[]{:S(2)}) %collective-permute-start.4) | collective-permute-done | bytes 32800 | tf_op jit(solution)/shard_map/ppermute | solution.py:13
  61.4 0.1 concatenate.32
  61.5 0.0 all-to-all-done
  61.5 0.4 fusion.11
  61.9 4.9 %multiply_convert_fusion = (bf16[768,512]{1,0:T(8,128)(2,1)}, bf16[768,512]{1,0:T(8,128)(2,1)}) fusion(bf16[768,512]{1,0:T(8,128)(2,1)} %param.11, f32[768,512]{1,0:T(8,128)} %fusion.20, bf16[512,512]{1,0:T(8,128)(2,1)} %param.13, f32[768,512]{1,0:T(8,128)} %fusion.21, f32[768,512]{1,0:T(8,128)S(1)} %fusion.11, bf16[768,64]{0,1:T(8,128)(2,1)S(1)} %bitcast.65, ...), kind=kOutput, calls=%fused_computation.20 | convolution fusion | flops 459669504 | bytes 7770116 | tf_op jit(solution)/shard_map/dot_general | solution.py:68
  66.8 1.9 divide_convert_fusion
  68.7 0.9 fusion.5
  69.5 0.9 fusion.23
  70.5 3.2 %fusion.22 = f32[768,512]{1,0:T(8,128)} fusion(bf16[768,768]{1,0:T(8,128)(2,1)} %bitcast.70, bf16[768,512]{1,0:T(8,128)(2,1)S(1)} %divide_convert_fusion), kind=kOutput, calls=%fused_computation.56 | convolution fusion | flops 603979776 | bytes 3538944 | tf_op jit(solution)/shard_map/dot_general | solution.py:83
  73.7 3.3 %all-to-all-start.1 = ((bf16[8,8,512]{2,1,0:T(8,128)(2,1)}), bf16[8,8,512]{2,1,0:T(8,128)(2,1)S(1)}, u32[]{:S(2)}, u32[]{:S(2)}) async-start(bf16[8,8,512]{2,1,0:T(8,128)(2,1)} %fusion.5), calls=%async_computation.1 | async-start | bytes 131072 | tf_op jit(solution)/shard_map/all_to_all | solution.py:89
  77.0 0.0 all-reduce.3.cloned.1.call-start
  77.1 0.7 all-reduce.3.cloned.1.call-update
  77.8 2.3 %convolution_add_fusion = f32[768,512]{1,0:T(8,128)S(1)} fusion(f32[768,512]{1,0:T(8,128)} %fusion.22, bf16[768,512]{1,0:T(8,128)(2,1)} %get-tuple-element.125, bf16[512,512]{1,0:T(8,128)(2,1)S(1)} %copy-done.1), kind=kOutput, calls=%fused_computation.24 | convolution fusion | flops 403046400 | bytes 4456448 | tf_op jit(solution)/shard_map/dot_general | solution.py:78
  80.0 128.6 %all-reduce.3.cloned.1.call-done = f32[64,512]{1,0:T(8,128)} async-done(((f32[64,512]{1,0:T(8,128)}), f32[64,512]{1,0:T(8,128)}) %all-reduce.3.cloned.1.call-update) | async-done | bytes 131088
  208.7 0.7 constant_dynamic-slice_fusion.1
  209.4 0.0 all-to-all-done.1
  209.4 1.6 scatter_custom_fusion
  211.0 1.0 convert_element_type.66
  (36 shorter events, 0.4 us)
Async XLA Ops:
  7.2 1.4 copy-start
  9.2 14.3 %collective-permute-start = (bf16[2,512]{1,0:T(2,128)(2,1)S(1)}, bf16[2,512]{1,0:T(2,128)(2,1)S(1)}, u32[]{:S(2)}, u32[]{:S(2)}) collective-permute-start(bf16[2,512]{1,0:T(2,128)(2,1)S(1)} %broadcast_select_fusion), channel_id=1, source_target_pairs={{0,31},{1,0},{2,1},{3,2},{4,3},{5,4},{6,5},{7,6},{8,7},{9,8},{10,9... | collective-permute-start | bytes 6152 | tf_op jit(solution)/shard_map/ppermute | solution.py:13
  18.5 43.0 %all-to-all-start = ((bf16[8,8,512]{2,1,0:T(8,128)(2,1)}), bf16[8,8,512]{2,1,0:T(8,128)(2,1)S(1)}, u32[]{:S(2)}, u32[]{:S(2)}) async-start(bf16[8,8,512]{2,1,0:T(8,128)(2,1)} %bitcast_select_fusion), calls=%async_computation | async-start | bytes 131072 | tf_op jit(solution)/shard_map/all_to_all | solution.py:58
  23.6 27.4 %collective-permute-start.1 = (bf16[4,512]{1,0:T(4,128)(2,1)S(1)}, bf16[4,512]{1,0:T(4,128)(2,1)S(1)}, u32[]{:S(2)}, u32[]{:S(2)}) collective-permute-start(bf16[4,512]{1,0:T(4,128)(2,1)S(1)} %pad_maximum_fusion.2), channel_id=1, source_target_pairs={{0,30},{1,31},{2,0},{3,1},{4,2},{5,3},{6,4},{7,5},{8,6},{9,7},{10,... | collective-permute-start | bytes 12296 | tf_op jit(solution)/shard_map/ppermute | solution.py:13
  51.0 1.0 copy-start.3
  51.0 4.6 %collective-permute-start.2 = (bf16[8,512]{1,0:T(8,128)(2,1)S(1)}, bf16[8,512]{1,0:T(8,128)(2,1)S(1)}, u32[]{:S(2)}, u32[]{:S(2)}) collective-permute-start(bf16[8,512]{1,0:T(8,128)(2,1)S(1)} %pad_maximum_fusion.1), channel_id=1, source_target_pairs={{0,28},{1,29},{2,30},{3,31},{4,0},{5,1},{6,2},{7,3},{8,4},{9,5},{1... | collective-permute-start | bytes 24584 | tf_op jit(solution)/shard_map/ppermute | solution.py:13
  52.0 3.7 %copy-start.1 = (bf16[512,512]{1,0:T(8,128)(2,1)S(1)}, bf16[512,512]{1,0:T(8,128)(2,1)}, u32[]{:S(2)}) copy-start(bf16[512,512]{1,0:T(8,128)(2,1)} %param.12) | copy-start | bytes 1572868
  53.9 4.2 %copy-start.4 = (s32[2]{0:T(128)S(1)}, s32[2]{0:T(128)}, u32[]{:S(2)}) copy-start(s32[2]{0:T(128)} %param.17) | copy-start | bytes 28
  53.9 4.3 %copy-start.2 = (s32[768]{0:T(1024)S(1)}, s32[768]{0:T(1024)}, u32[]{:S(2)}) copy-start(s32[768]{0:T(1024)} %param.15) | copy-start | bytes 9220
  55.6 1.8 collective-permute-start.3
  57.5 4.0 %collective-permute-start.4 = (bf16[32,512]{1,0:T(8,128)(2,1)S(1)}, bf16[32,512]{1,0:T(8,128)(2,1)S(1)}, u32[]{:S(2)}, u32[]{:S(2)}) collective-permute-start(bf16[32,512]{1,0:T(8,128)(2,1)S(1)} %concatenate.31), channel_id=1, source_target_pairs={{0,16},{1,17},{2,18},{3,19},{4,20},{5,21},{6,22},{7,23},{8,24},{9,... | collective-permute-start | bytes 98312 | tf_op jit(solution)/shard_map/ppermute | solution.py:13
  73.7 135.7 %all-to-all-start.1 = ((bf16[8,8,512]{2,1,0:T(8,128)(2,1)}), bf16[8,8,512]{2,1,0:T(8,128)(2,1)S(1)}, u32[]{:S(2)}, u32[]{:S(2)}) async-start(bf16[8,8,512]{2,1,0:T(8,128)(2,1)} %fusion.5), calls=%async_computation.1 | async-start | bytes 131072 | tf_op jit(solution)/shard_map/all_to_all | solution.py:89
  77.0 131.6 %all-reduce.3.cloned.1.call-start = ((), (), s32[]{:S(2)}) async-start(), calls=%async_computation.2 | async-start | bytes 262144
Sparse Core Ops, SparseCore 0:
  83.4 125.2 all-reduce.2
